TPU v7x, 128 devices: a whole 4x4x4 slice. The times are simulated.
128 devices in a mesh: wide: 32 (over x, z, core), narrow: 4 (over y).
Axes of the slice: x: 4, y: 4, z: 4, core: 2. Of those that a mesh axis runs over, the one named last changes fastest.
Arguments:
- member: bfloat16 [2048, 8192], P('narrow', 'wide'), may hold values from 0.01 to 300, as said below
Outputs:
- transition: float32 [8192, 8192], P('wide', 'narrow')
- stationary: float32 [8192], P('wide')
Inputs may be any that keep to these rules, and one draw needn't show every extreme that they name: `member`: strictly positive weights.
All inputs are finite; a program needn't handle non-finite values.
Results may differ from a plain program's by a relative error of at most 0.0003.
Values may be sent and summed in bfloat16 or wider, within the bound.
No kernel may reach another device: no remote copies, remote signals or barrier semaphores. Data moves between devices by JAX's collectives and lax.ppermute only.
A program may use at most 128 MiB of HBM per device.

v0:
```python
import jax
import jax.numpy as jnp
from jax import lax
from jax.sharding import PartitionSpec as P

STATES = 8192
TAU = 64
ITERS = 3


def passed_along(block, axis, distance):
    devices = range(lax.axis_size(axis))
    route = [(i - distance, i) for i in devices if i - distance in devices]
    return lax.ppermute(block, axis, route)


def contract_frames(left, right):
    return lax.dot_general(
        left, right, (((0,), (0,)), ((), ())), preferred_element_type=jnp.float32
    )


def shards(member):
    rim = passed_along(member[:TAU], "narrow", -1)
    lagged = jnp.concatenate([member[TAU:], rim], axis=0)
    frame_part = jnp.sum(lagged, axis=1, dtype=jnp.float32)
    frame_totals = lax.psum(frame_part, "wide")
    visit_part = jnp.dot(frame_totals, member.astype(jnp.float32), precision=lax.Precision.HIGHEST)
    stacked = jnp.stack([member, lagged])
    piece = lax.all_gather(stacked, "wide", axis=2, tiled=True)
    partial_value = contract_frames(member, piece[1]) + contract_frames(lagged, piece[0])
    counts = lax.psum_scatter(partial_value, "narrow", scatter_dimension=1, tiled=True)
    row_now, visit_rows = lax.psum((jnp.sum(counts, axis=1), visit_part), "narrow")
    visit_all = lax.all_gather(visit_rows, "wide", axis=0, tiled=True)
    width_cols = counts.shape[1]
    col_start = lax.axis_index("narrow") * width_cols
    visit_cols = lax.dynamic_slice_in_dim(visit_all, col_start, width_cols)
    estimate = counts
    for step in range(ITERS):
        all_rows = lax.all_gather(row_now, "wide", axis=0, tiled=True)
        col_now = lax.dynamic_slice_in_dim(all_rows, col_start, width_cols)
        ratio_rows = visit_rows / row_now
        ratio_cols = visit_cols / col_now
        estimate = counts / (ratio_rows[:, None] + ratio_cols[None, :])
        row_now = lax.psum(jnp.sum(estimate, axis=1), "narrow")
    transition = STATES * estimate / row_now[:, None]
    grand = lax.psum(jnp.sum(row_now), "wide")
    stationary = STATES * row_now / grand
    return (transition, stationary)


def solution(mesh):
    return jax.shard_map(
        shards,
        mesh=mesh,
        in_specs=(P("narrow", "wide"),),
        out_specs=(P("wide", "narrow"), P("wide")),
        check_vma=False,
    )
```

profile of v0, /device:TPU:1, one launch (start us, length us, event | category | flops | bytes accessed | tf_op | source)
XLA Modules:
  0.0 404.0 jit_solution(7120169739386829088)
XLA Ops:
  7.2 0.0 copy-start.1
  7.2 0.0 all-gather.6.cloned.1.call-start
  7.2 0.8 slice.13
  8.0 1.3 collective-permute-start
  9.3 1.0 slice.12
  10.3 3.1 collective-permute-done
  13.3 1.8 pad_maximum_fusion
  15.1 0.0 all-gather.6.cloned.1.call-update
  15.2 0.0 reduce-scatter.2.cloned.1.call-start
  15.2 84.3 %all-gather.6.cloned.1.call-done = bf16[2,512,8192]{2,1,0:T(8,128)(2,1)} async-done(((bf16[2,512,256]{2,1,0:T(8,128)(2,1)}), bf16[2,512,8192]{2,1,0:T(8,128)(2,1)}) %all-gather.6.cloned.1.call-update) | async-done | bytes 16777232 | tf_op jit(solution)/shard_map/all_gather | solution.py:30
  99.5 0.0 copy-done.1
  99.5 5.8 %convolution_bitcast_fusion = f32[256,8192]{0,1:T(8,128)S(1)} fusion(bf16[512,256]{1,0:T(8,128)(2,1)S(1)} %copy-done.1, bf16[2,512,8192]{2,1,0:T(8,128)(2,1)} %all-gather.6.cloned.1.call-done), kind=kOutput, calls=%fused_computation | convolution fusion | flops 2147483648 | bytes 17039360 | tf_op jit(solution)/shard_map/dot_general | solution.py:18
  105.3 10.0 %convolution_add_fusion = f32[256,8192]{0,1:T(8,128)} fusion(f32[256,8192]{0,1:T(8,128)S(1)} %convolution_bitcast_fusion, bf16[2,512,8192]{2,1,0:T(8,128)(2,1)} %all-gather.6.cloned.1.call-done, bf16[64,256]{1,0:T(8,128)(2,1)S(1)} %collective-permute-done, bf16[448,256]{1,0:T(8,128)(2,1)S(1)} %slice.12), kind=kOutput, calls=%fused_computation.1 | convolution fusion | flops 2150105088 | bytes 25427968 | tf_op jit(solution)/shard_map/dot_general | solution.py:18
  115.2 0.0 reduce-scatter.2.cloned.1.call-update
  115.3 0.1 convert_reduce_fusion
  115.4 62.3 %psum.49 = f32[512]{0:T(512)S(1)} all-reduce(f32[512]{0:T(512)S(1)} %convert_reduce_fusion), channel_id=1, replica_groups=mesh['wide'=32,'narrow'=4] {'wide'}, use_global_device_ids=true, to_apply=%region_2.0 | all-reduce | flops 512 | bytes 4096 | tf_op jit(solution)/shard_map/psum | solution.py:27
  177.7 0.2 fusion.5
  177.9 17.7 %reduce-scatter.2.cloned.1.call-done = f32[256,2048]{0,1:T(8,128)} async-done(((f32[256,8192]{0,1:T(8,128)}), f32[256,2048]{0,1:T(8,128)}) %reduce-scatter.2.cloned.1.call-update) | async-done | bytes 2097168 | tf_op jit(solution)/shard_map/reduce_scatter | solution.py:32
  195.6 0.0 copy-start
  195.6 2.0 reduce_sum.55
  197.6 6.5 %all-reduce = (f32[256]{0:T(256)S(1)}, f32[256]{0:T(256)S(1)}) all-reduce(f32[256]{0:T(256)S(1)} %reduce_sum.55, f32[256]{0:T(256)S(1)} %bitcast.35), channel_id=1, replica_groups=mesh['wide'=32,'narrow'=4] {'narrow'}, use_global_device_ids=true, to_apply=%region_5.0 | all-reduce | flops 512 | bytes 4096 | tf_op jit(solution)/shard_map/psum | solution.py:33
  204.2 27.0 %all-gather = f32[32,1,256]{2,1,0:T(1,128)S(1)} all-gather(f32[1,1,256]{2,1,0:T(1,128)S(1)} %bitcast.31), channel_id=1, replica_groups=mesh['wide'=32,'narrow'=4] {'wide'}, dimensions={0}, use_global_device_ids=true | all-gather | bytes 33792 | tf_op jit(solution)/shard_map/all_gather | solution.py:34
  231.2 23.6 %all-gather.1 = f32[32,1,256]{2,1,0:T(1,128)S(1)} all-gather(f32[1,1,256]{2,1,0:T(1,128)S(1)} %bitcast.36), channel_id=1, replica_groups=mesh['wide'=32,'narrow'=4] {'wide'}, dimensions={0}, use_global_device_ids=true | all-gather | bytes 33792 | tf_op jit(solution)/shard_map/all_gather | solution.py:40
  254.8 0.0 copy-done
  254.8 0.4 fusion
  255.1 6.9 %psum.52 = f32[256]{0:T(256)S(1)} all-reduce(f32[256]{0:T(256)S(1)} %fusion), channel_id=1, replica_groups=mesh['wide'=32,'narrow'=4] {'narrow'}, use_global_device_ids=true, to_apply=%region_7.0 | all-reduce | flops 256 | bytes 2048 | tf_op jit(solution)/shard_map/psum | solution.py:45
  262.0 24.1 %all-gather.2 = f32[32,1,256]{2,1,0:T(1,128)S(1)} all-gather(f32[1,1,256]{2,1,0:T(1,128)S(1)} %bitcast.33), channel_id=1, replica_groups=mesh['wide'=32,'narrow'=4] {'wide'}, dimensions={0}, use_global_device_ids=true | all-gather | bytes 33792 | tf_op jit(solution)/shard_map/all_gather | solution.py:40
  286.1 0.4 fusion.1
  286.5 6.6 %psum.53 = f32[256]{0:T(256)S(1)} all-reduce(f32[256]{0:T(256)S(1)} %fusion.1), channel_id=1, replica_groups=mesh['wide'=32,'narrow'=4] {'narrow'}, use_global_device_ids=true, to_apply=%region_9.0 | all-reduce | flops 256 | bytes 2048 | tf_op jit(solution)/shard_map/psum | solution.py:45
  293.0 25.6 %all-gather.3 = f32[32,1,256]{2,1,0:T(1,128)S(1)} all-gather(f32[1,1,256]{2,1,0:T(1,128)S(1)} %bitcast.32), channel_id=1, replica_groups=mesh['wide'=32,'narrow'=4] {'wide'}, dimensions={0}, use_global_device_ids=true | all-gather | bytes 33792 | tf_op jit(solution)/shard_map/all_gather | solution.py:40
  318.6 0.4 fusion.2
  319.0 6.9 %psum.54 = f32[256]{0:T(256)S(1)} all-reduce(f32[256]{0:T(256)S(1)} %fusion.2), channel_id=1, replica_groups=mesh['wide'=32,'narrow'=4] {'narrow'}, use_global_device_ids=true, to_apply=%region_11.0 | all-reduce | flops 256 | bytes 2048 | tf_op jit(solution)/shard_map/psum | solution.py:45
  325.9 0.6 reduce_sum.59
  326.5 64.8 %psum.55 = f32[]{:T(128)} all-reduce(f32[]{:T(128)} %reduce_sum.59), channel_id=1, replica_groups=mesh['wide'=32,'narrow'=4] {'wide'}, use_global_device_ids=true, to_apply=%region_13.0 | all-reduce | flops 1 | bytes 8 | tf_op jit(solution)/shard_map/psum | solution.py:47
  391.3 1.2 multiply_divide_fusion.1
  392.5 1.8 multiply_divide_fusion
  394.3 2.9 copy.6
  (7 shorter events, 0.1 us)
Async XLA Ops:
  7.2 92.3 %copy-start.1 = (bf16[512,256]{1,0:T(8,128)(2,1)S(1)}, bf16[512,256]{1,0:T(8,128)(2,1)}, u32[]{:S(2)}) copy-start(bf16[512,256]{1,0:T(8,128)(2,1)} %param.1) | copy-start | bytes 786436
  7.2 92.3 %all-gather.6.cloned.1.call-start = ((), (), s32[]{:S(2)}) async-start(), calls=%async_computation.1 | async-start | bytes 17301504 | tf_op jit(solution)/shard_map/all_gather | solution.py:30
  8.0 5.3 %collective-permute-start = (bf16[64,256]{1,0:T(8,128)(2,1)S(1)}, bf16[64,256]{1,0:T(8,128)(2,1)S(1)}, u32[]{:S(2)}, u32[]{:S(2)}) collective-permute-start(bf16[64,256]{1,0:T(8,128)(2,1)S(1)} %slice.13), channel_id=1, source_target_pairs={{1,0},{2,1},{3,2},{5,4},{6,5},{7,6},{9,8},{10,9},{11,10},{13,12},{... | collective-permute-start | bytes 98312 | tf_op jit(solution)/shard_map/ppermute | solution.py:14
  15.2 180.4 %reduce-scatter.2.cloned.1.call-start = ((), (), s32[]{:S(2)}) async-start(), calls=%async_computation.2 | async-start | bytes 10485760 | tf_op jit(solution)/shard_map/reduce_scatter | solution.py:32
  195.6 59.2 %copy-start = (f32[256,2048]{0,1:T(8,128)S(1)}, f32[256,2048]{0,1:T(8,128)}, u32[]{:S(2)}) copy-start(f32[256,2048]{0,1:T(8,128)} %reduce-scatter.2.cloned.1.call-done) | copy-start | bytes 6291460
Sparse Core Ops, SparseCore 0:
  15.3 84.1 all-gather.5
  115.4 80.1 reduce-scatter.1
where the time goes:
time: 405 us; the launch traced here: 404 us
  blocking collectives  254 us (63%)
  waiting for transfers between devices  105 us (26%)
  matrix products  15.9 us (4%)
  between operations  14.1 us (3%)
  other arithmetic  8.7 us (2%)
  local copies, waits for them, and re-layouts  4.64 us (1%)
    all_gather x1, waiting for transfers between devices, shards(): piece = lax.all_gather(stacked, 'wide', axis=2, tiled=True)  84.3 us
    all_gather x3, blocking collectives, shards(): all_rows = lax.all_gather(row_now, 'wide', axis=0, tiled=True)  73.2 us
    psum x1, blocking collectives, shards(): grand = lax.psum(jnp.sum(row_now), 'wide')  64.8 us
    psum x1, blocking collectives, shards(): frame_totals = lax.psum(frame_part, 'wide')  62.3 us
    all_gather x1, blocking collectives, shards(): visit_all = lax.all_gather(visit_rows, 'wide', axis=0, tiled=True)  27 us
    psum x3, blocking collectives, shards(): row_now = lax.psum(jnp.sum(estimate, axis=1), 'narrow')  20.3 us
    reduce_scatter x1, waiting for transfers between devices, shards(): lax.psum_scatter(partial_value, 'narrow', scatter_dimension=1, tiled=True)  17.7 us
    dot_general x2, matrix products, contract_frames(): lax.dot_general(left, right, (((0,), (0,)), ((), ())), preferred_element_...  15.7 us
  transfers between devices with their start and end apart: 3, of which 3 were waited for; matrix products, arithmetic and copies ran while one was open for 0% of the time, Pallas kernels for 0%

commit v1 on v0

--- a/solution.py
+++ b/solution.py
@@ -31,7 +31,10 @@
     partial_value = contract_frames(member, piece[1]) + contract_frames(lagged, piece[0])
     counts = lax.psum_scatter(partial_value, "narrow", scatter_dimension=1, tiled=True)
     row_now, visit_rows = lax.psum((jnp.sum(counts, axis=1), visit_part), "narrow")
-    visit_all = lax.all_gather(visit_rows, "wide", axis=0, tiled=True)
+    reached = lax.axis_size("wide")
+    seen_now = jnp.stack([visit_rows] * reached)
+    outer = lax.all_to_all(seen_now, "wide", split_axis=0, concat_axis=0)
+    visit_all = jnp.concatenate(outer, axis=0)
     width_cols = counts.shape[1]
     col_start = lax.axis_index("narrow") * width_cols
     visit_cols = lax.dynamic_slice_in_dim(visit_all, col_start, width_cols)

time: 405 us -> 389 us (0.960)
  blocking collectives: 254 us -> 228 us
  starting transfers between devices: 1.36 us -> 11.1 us
    all_gather x1 -> x0, blocking collectives: 27 us -> none  [shards(): visit_all = lax.all_gather(visit_rows, 'wide', axis=0, tiled=True)]
    all_to_all x0 -> x1, starting transfers between devices: none -> 9.74 us  [shards(): outer = lax.all_to_all(seen_now, 'wide', split_axis=0, concat_axis=0)]
  transfers between devices with their start and end apart: 3 -> 4, of which waited for: 3 -> 3; matrix products, arithmetic and copies ran while one was open for 0% -> 0% of each run, Pallas kernels for 0% -> 0%
where the time goes in v1:
time: 389 us; the launch traced here: 388 us
  blocking collectives  228 us (59%)
  waiting for transfers between devices  105 us (27%)
  matrix products  15.9 us (4%)
  between operations  14.1 us (4%)
  starting transfers between devices  11.1 us (3%)
  other arithmetic  8.7 us (2%)
  local copies, waits for them, and re-layouts  5.28 us (1%)
    all_gather x1, waiting for transfers between devices, shards(): piece = lax.all_gather(stacked, 'wide', axis=2, tiled=True)  84.3 us
    all_gather x3, blocking collectives, shards(): all_rows = lax.all_gather(row_now, 'wide', axis=0, tiled=True)  74.3 us
    psum x1, blocking collectives, shards(): grand = lax.psum(jnp.sum(row_now), 'wide')  64.8 us
    psum x1, blocking collectives, shards(): frame_totals = lax.psum(frame_part, 'wide')  62.3 us
    psum x3, blocking collectives, shards(): row_now = lax.psum(jnp.sum(estimate, axis=1), 'narrow')  20.4 us
    reduce_scatter x1, waiting for transfers between devices, shards(): lax.psum_scatter(partial_value, 'narrow', scatter_dimension=1, tiled=True)  17.7 us
    dot_general x2, matrix products, contract_frames(): lax.dot_general(left, right, (((0,), (0,)), ((), ())), preferred_element_...  15.7 us
    all_to_all x1, starting transfers between devices, shards(): outer = lax.all_to_all(seen_now, 'wide', split_axis=0, concat_axis=0)  9.74 us
  transfers between devices with their start and end apart: 4, of which 3 were waited for; matrix products, arithmetic and copies ran while one was open for 0% of the time, Pallas kernels for 0%

profile of v1, /device:TPU:1, one launch (start us, length us, event | category | flops | bytes accessed | tf_op | source)
XLA Modules:
  0.0 388.5 jit_solution(3196518839189607367)
XLA Ops:
  7.2 0.0 copy-start.1
  7.2 0.0 all-gather.5.cloned.1.call-start
  7.2 0.8 slice.13
  8.0 1.3 collective-permute-start
  9.3 1.0 slice.12
  10.3 3.1 collective-permute-done
  13.3 1.8 pad_maximum_fusion
  15.1 0.0 all-gather.5.cloned.1.call-update
  15.2 0.0 reduce-scatter.2.cloned.1.call-start
  15.2 84.3 %all-gather.5.cloned.1.call-done = bf16[2,512,8192]{2,1,0:T(8,128)(2,1)} async-done(((bf16[2,512,256]{2,1,0:T(8,128)(2,1)}), bf16[2,512,8192]{2,1,0:T(8,128)(2,1)}) %all-gather.5.cloned.1.call-update) | async-done | bytes 16777232 | tf_op jit(solution)/shard_map/all_gather | solution.py:30
  99.5 0.0 copy-done.1
  99.5 5.8 %convolution_bitcast_fusion = f32[256,8192]{0,1:T(8,128)S(1)} fusion(bf16[512,256]{1,0:T(8,128)(2,1)S(1)} %copy-done.1, bf16[2,512,8192]{2,1,0:T(8,128)(2,1)} %all-gather.5.cloned.1.call-done), kind=kOutput, calls=%fused_computation | convolution fusion | flops 2147483648 | bytes 17039360 | tf_op jit(solution)/shard_map/dot_general | solution.py:18
  105.3 10.0 %convolution_add_fusion = f32[256,8192]{0,1:T(8,128)} fusion(f32[256,8192]{0,1:T(8,128)S(1)} %convolution_bitcast_fusion, bf16[2,512,8192]{2,1,0:T(8,128)(2,1)} %all-gather.5.cloned.1.call-done, bf16[64,256]{1,0:T(8,128)(2,1)S(1)} %collective-permute-done, bf16[448,256]{1,0:T(8,128)(2,1)S(1)} %slice.12), kind=kOutput, calls=%fused_computation.1 | convolution fusion | flops 2150105088 | bytes 25427968 | tf_op jit(solution)/shard_map/dot_general | solution.py:18
  115.2 0.0 reduce-scatter.2.cloned.1.call-update
  115.3 0.1 convert_reduce_fusion
  115.4 62.3 %psum.49 = f32[512]{0:T(512)S(1)} all-reduce(f32[512]{0:T(512)S(1)} %convert_reduce_fusion), channel_id=1, replica_groups=mesh['wide'=32,'narrow'=4] {'wide'}, use_global_device_ids=true, to_apply=%region_2.0 | all-reduce | flops 512 | bytes 4096 | tf_op jit(solution)/shard_map/psum | solution.py:27
  177.7 0.2 fusion.5
  177.9 17.7 %reduce-scatter.2.cloned.1.call-done = f32[256,2048]{0,1:T(8,128)} async-done(((f32[256,8192]{0,1:T(8,128)}), f32[256,2048]{0,1:T(8,128)}) %reduce-scatter.2.cloned.1.call-update) | async-done | bytes 2097168 | tf_op jit(solution)/shard_map/reduce_scatter | solution.py:32
  195.6 0.0 copy-start
  195.6 2.0 reduce_sum.55
  197.6 6.5 %all-reduce = (f32[256]{0:T(256)S(1)}, f32[256]{0:T(256)S(1)}) all-reduce(f32[256]{0:T(256)S(1)} %reduce_sum.55, f32[256]{0:T(256)S(1)} %bitcast.33), channel_id=1, replica_groups=mesh['wide'=32,'narrow'=4] {'narrow'}, use_global_device_ids=true, to_apply=%region_5.0 | all-reduce | flops 512 | bytes 4096 | tf_op jit(solution)/shard_map/psum | solution.py:33
  204.2 0.6 stack.11
  204.8 9.7 %all-to-all-start = ((f32[32,1,256]{2,1,0:T(1,128)}), f32[32,1,256]{2,1,0:T(1,128)S(1)}, u32[]{:S(2)}, u32[]{:S(2)}) async-start(f32[32,1,256]{2,1,0:T(1,128)} %stack.11), calls=%async_computation.1 | async-start | bytes 65536 | tf_op jit(solution)/shard_map/all_to_all | solution.py:36
  214.6 24.6 %all-gather = f32[32,1,256]{2,1,0:T(1,128)S(1)} all-gather(f32[1,1,256]{2,1,0:T(1,128)S(1)} %bitcast.34), channel_id=1, replica_groups=mesh['wide'=32,'narrow'=4] {'wide'}, dimensions={0}, use_global_device_ids=true | all-gather | bytes 33792 | tf_op jit(solution)/shard_map/all_gather | solution.py:43
  239.2 0.0 all-to-all-done
  239.2 0.0 copy-done
  239.2 0.4 fusion
  239.6 6.9 %psum.52 = f32[256]{0:T(256)S(1)} all-reduce(f32[256]{0:T(256)S(1)} %fusion), channel_id=1, replica_groups=mesh['wide'=32,'narrow'=4] {'narrow'}, use_global_device_ids=true, to_apply=%region_7.0 | all-reduce | flops 256 | bytes 2048 | tf_op jit(solution)/shard_map/psum | solution.py:48
  246.5 25.6 %all-gather.1 = f32[32,1,256]{2,1,0:T(1,128)S(1)} all-gather(f32[1,1,256]{2,1,0:T(1,128)S(1)} %bitcast.31), channel_id=1, replica_groups=mesh['wide'=32,'narrow'=4] {'wide'}, dimensions={0}, use_global_device_ids=true | all-gather | bytes 33792 | tf_op jit(solution)/shard_map/all_gather | solution.py:43
  272.1 0.4 fusion.1
  272.5 6.6 %psum.53 = f32[256]{0:T(256)S(1)} all-reduce(f32[256]{0:T(256)S(1)} %fusion.1), channel_id=1, replica_groups=mesh['wide'=32,'narrow'=4] {'narrow'}, use_global_device_ids=true, to_apply=%region_9.0 | all-reduce | flops 256 | bytes 2048 | tf_op jit(solution)/shard_map/psum | solution.py:48
  279.0 24.0 %all-gather.2 = f32[32,1,256]{2,1,0:T(1,128)S(1)} all-gather(f32[1,1,256]{2,1,0:T(1,128)S(1)} %bitcast.30), channel_id=1, replica_groups=mesh['wide'=32,'narrow'=4] {'wide'}, dimensions={0}, use_global_device_ids=true | all-gather | bytes 33792 | tf_op jit(solution)/shard_map/all_gather | solution.py:43
  303.1 0.4 fusion.2
  303.5 6.9 %psum.54 = f32[256]{0:T(256)S(1)} all-reduce(f32[256]{0:T(256)S(1)} %fusion.2), channel_id=1, replica_groups=mesh['wide'=32,'narrow'=4] {'narrow'}, use_global_device_ids=true, to_apply=%region_11.0 | all-reduce | flops 256 | bytes 2048 | tf_op jit(solution)/shard_map/psum | solution.py:48
  310.4 0.6 reduce_sum.59
  311.0 64.8 %psum.55 = f32[]{:T(128)} all-reduce(f32[]{:T(128)} %reduce_sum.59), channel_id=1, replica_groups=mesh['wide'=32,'narrow'=4] {'wide'}, use_global_device_ids=true, to_apply=%region_13.0 | all-reduce | flops 1 | bytes 8 | tf_op jit(solution)/shard_map/psum | solution.py:50
  375.8 1.2 multiply_divide_fusion.1
  377.0 1.8 multiply_divide_fusion
  378.8 2.9 copy.6
  (7 shorter events, 0.1 us)
Async XLA Ops:
  7.2 92.3 %copy-start.1 = (bf16[512,256]{1,0:T(8,128)(2,1)S(1)}, bf16[512,256]{1,0:T(8,128)(2,1)}, u32[]{:S(2)}) copy-start(bf16[512,256]{1,0:T(8,128)(2,1)} %param.1) | copy-start | bytes 786436
  7.2 92.3 %all-gather.5.cloned.1.call-start = ((), (), s32[]{:S(2)}) async-start(), calls=%async_computation.2 | async-start | bytes 17301504 | tf_op jit(solution)/shard_map/all_gather | solution.py:30
  8.0 5.3 %collective-permute-start = (bf16[64,256]{1,0:T(8,128)(2,1)S(1)}, bf16[64,256]{1,0:T(8,128)(2,1)S(1)}, u32[]{:S(2)}, u32[]{:S(2)}) collective-permute-start(bf16[64,256]{1,0:T(8,128)(2,1)S(1)} %slice.13), channel_id=1, source_target_pairs={{1,0},{2,1},{3,2},{5,4},{6,5},{7,6},{9,8},{10,9},{11,10},{13,12},{... | collective-permute-start | bytes 98312 | tf_op jit(solution)/shard_map/ppermute | solution.py:14
  15.2 180.4 %reduce-scatter.2.cloned.1.call-start = ((), (), s32[]{:S(2)}) async-start(), calls=%async_computation.3 | async-start | bytes 10485760 | tf_op jit(solution)/shard_map/reduce_scatter | solution.py:32
  195.6 43.6 %copy-start = (f32[256,2048]{0,1:T(8,128)S(1)}, f32[256,2048]{0,1:T(8,128)}, u32[]{:S(2)}) copy-start(f32[256,2048]{0,1:T(8,128)} %reduce-scatter.2.cloned.1.call-done) | copy-start | bytes 6291460
  204.8 34.4 %all-to-all-start = ((f32[32,1,256]{2,1,0:T(1,128)}), f32[32,1,256]{2,1,0:T(1,128)S(1)}, u32[]{:S(2)}, u32[]{:S(2)}) async-start(f32[32,1,256]{2,1,0:T(1,128)} %stack.11), calls=%async_computation.1 | async-start | bytes 65536 | tf_op jit(solution)/shard_map/all_to_all | solution.py:36
Sparse Core Ops, SparseCore 0:
  15.3 84.1 all-gather.4
  115.4 80.1 reduce-scatter.1
